TPU v7x, 32 devices: a whole 2x2x4 slice. The times are simulated.
32 devices in a mesh: dp: 8 (over z, x), tensor: 4 (over y, core).
Axes of the slice: x: 2, y: 2, z: 4, core: 2. Of those that a mesh axis runs over, the one named last changes fastest.
Arguments:
- hidden_in: bfloat16 [16384, 768], P('dp'), may hold values from -6 to 6
- doc_ids: int32 [16384], P('dp'), may hold values from 0 to 7, as said below
- ln1_gain: float32 [768], replicated, may hold values from 0.5 to 1.5
- ln1_bias: float32 [768], replicated, may hold values from -1.25 to 1.25
- w_qkv: bfloat16 [768, 3, 12, 64], P(None, None, 'tensor'), may hold values from -0.3125 to 0.3125
- b_qv: float32 [2, 12, 64], P(None, 'tensor'), may hold values from -1.75 to 1.75
- w_out: bfloat16 [12, 64, 768], P('tensor'), may hold values from -0.875 to 0.875
- b_out: float32 [768], replicated, may hold values from -1.25 to 1.25
- ln2_gain: float32 [768], replicated, may hold values from 0.5 to 1.5
- ln2_bias: float32 [768], replicated, may hold values from -1.25 to 1.25
- w_fc: bfloat16 [768, 3072], P(None, 'tensor'), may hold values from -0.21875 to 0.21875
- b_fc: float32 [24, 128], P('tensor'), may hold values from -1.75 to 1.75
- w_proj: bfloat16 [3072, 768], P('tensor'), may hold values from -0.109375 to 0.109375
- b_proj: float32 [768], replicated, may hold values from -1.25 to 1.25
- grad_out: bfloat16 [16384, 768], P('dp'), may hold values from -6 to 6
Outputs:
- block_out: bfloat16 [16384, 768], P('dp')
- grad_in: float32 [16384, 768], P('dp')
- grad_ln1_gain: float32 [768], P('dp')
- grad_ln1_bias: float32 [768], P('dp')
- grad_w_qkv: float32 [768, 3, 12, 64], P('dp', None, 'tensor')
- grad_b_qv: float32 [2, 12, 64], P(None, 'tensor', 'dp')
- grad_w_out: float32 [12, 64, 768], P('tensor', None, 'dp')
- grad_b_out: float32 [768], P('dp')
- grad_ln2_gain: float32 [768], P('dp')
- grad_ln2_bias: float32 [768], P('dp')
- grad_w_fc: float32 [768, 3072], P('dp', 'tensor')
- grad_b_fc: float32 [24, 128], P('tensor', 'dp')
- grad_w_proj: float32 [3072, 768], P('tensor', 'dp')
- grad_b_proj: float32 [768], P('dp')
Inputs may be any that keep to these rules, and one draw needn't show every extreme that they name: `doc_ids`: each aligned block of 2048 tokens (one index of dp) holds either 2048 // 1024 sequences of 1024 tokens or 8 sequences of 256 tokens, numbered from 0 in order; exactly half of the blocks hold the long ones.
All inputs are finite; a program needn't handle non-finite values.
Results may differ from a plain program's by a relative error of at most 0.015.
The roundings to bfloat16 on the way count: a program that leaves them out, or rounds other values in their place, can miss the bound.
Values may be sent and summed in bfloat16 or wider, within the bound.
No kernel may reach another device: no remote copies, remote signals or barrier semaphores. Data moves between devices by JAX's collectives and lax.ppermute only.
A program may use at most 192 MiB of HBM per device.

v0:
```python
import math
import jax
import jax.numpy as jnp
from jax import lax
from jax.sharding import PartitionSpec as P

EPSILON = 1e-05
MASKED = -1e30


def normalize(values):
    row_mean = jnp.mean(values, axis=-1, keepdims=True)
    centered = values - row_mean
    inv_std = lax.rsqrt(jnp.mean(centered * centered, axis=-1, keepdims=True) + EPSILON)
    return (centered * inv_std, inv_std)


def norm_back(grad_normed, normed, inv_std, gain_vec):
    scaled = grad_normed * gain_vec
    return inv_std * (
        scaled
        - jnp.mean(scaled, axis=-1, keepdims=True)
        - normed * jnp.mean(scaled * normed, axis=-1, keepdims=True)
    )


def masked_scores(queries, key_rows, row_ids, key_ids, start_row, scale_factor):
    scores = (
        jnp.einsum("qhd,khd->hqk", queries, key_rows, preferred_element_type=jnp.float32)
        * scale_factor
    )
    row_pos = start_row + jnp.arange(queries.shape[0])
    key_pos = jnp.arange(key_rows.shape[0])
    allowed = (row_pos[:, None] >= key_pos[None, :]) & (row_ids[:, None] == key_ids[None, :])
    return jnp.where(allowed[None], scores, MASKED)


def body(
    hidden_in,
    doc_ids,
    ln1_gain,
    ln1_bias,
    w_qkv,
    b_qv,
    w_out,
    b_out,
    ln2_gain,
    ln2_bias,
    w_fc,
    b_fc,
    w_proj,
    b_proj,
    grad_out,
):
    row_count, model_width = hidden_in.shape
    local_heads = w_qkv.shape[2]
    head_dim = w_qkv.shape[3]
    local_width = local_heads * head_dim
    hidden_units = w_fc.shape[1]
    scale_factor = 1.0 / math.sqrt(head_dim)
    block_rows = min(512, row_count)
    block_count = row_count // block_rows
    qkv_matrix = w_qkv.reshape(model_width, 3 * local_width)
    out_matrix = w_out.reshape(local_width, model_width)
    x_float = hidden_in.astype(jnp.float32)
    normed_one, inv_one = normalize(x_float)
    first_in = (normed_one * ln1_gain + ln1_bias).astype(jnp.bfloat16)
    projected = jnp.dot(first_in, qkv_matrix, preferred_element_type=jnp.float32).reshape(
        row_count, 3, local_heads, head_dim
    )
    queries = (projected[:, 0] + b_qv[0]).astype(jnp.bfloat16)
    key_rows = projected[:, 1].astype(jnp.bfloat16)
    value_rows = (projected[:, 2] + b_qv[1]).astype(jnp.bfloat16)
    attended_parts = []
    log_totals = []
    for block_index in range(block_count):
        start_row = block_index * block_rows
        end_row = start_row + block_rows
        scores = masked_scores(
            queries[start_row:end_row],
            key_rows[:end_row],
            doc_ids[start_row:end_row],
            doc_ids[:end_row],
            start_row,
            scale_factor,
        )
        row_max = jnp.max(scores, axis=-1, keepdims=True)
        exp_scores = jnp.exp(scores - row_max)
        row_total = jnp.sum(exp_scores, axis=-1, keepdims=True)
        weights_low = (exp_scores / row_total).astype(jnp.bfloat16)
        log_totals.append(row_max + jnp.log(row_total))
        attended_parts.append(
            jnp.einsum(
                "hqk,khd->qhd",
                weights_low,
                value_rows[:end_row],
                preferred_element_type=jnp.float32,
            )
        )
    attended = (
        jnp.concatenate(attended_parts, axis=0).reshape(row_count, local_width).astype(jnp.bfloat16)
    )
    branch_part = jnp.dot(attended, out_matrix, preferred_element_type=jnp.float32)
    branch = lax.psum(branch_part, "tensor") + b_out
    residual = x_float + branch
    normed_two, inv_two = normalize(residual)
    second_in = (normed_two * ln2_gain + ln2_bias).astype(jnp.bfloat16)
    pre_act = jnp.dot(second_in, w_fc, preferred_element_type=jnp.float32) + b_fc.reshape(
        hidden_units
    )
    act_value, gelu_back = jax.vjp(
        lambda pre_value: jax.nn.gelu(pre_value, approximate=True), pre_act
    )
    act_low = act_value.astype(jnp.bfloat16)
    mlp_part = jnp.dot(act_low, w_proj, preferred_element_type=jnp.float32)
    block_out = (
        residual + lax.psum(mlp_part.astype(jnp.bfloat16), "tensor").astype(jnp.float32) + b_proj
    )
    grad_float = grad_out.astype(jnp.float32)
    grad_w_proj = jnp.einsum("rf,rd->fd", act_low, grad_out, preferred_element_type=jnp.float32)
    grad_b_proj = jnp.sum(grad_float, axis=0)
    grad_act = jnp.einsum("rd,fd->rf", grad_out, w_proj, preferred_element_type=jnp.float32)
    grad_pre = gelu_back(grad_act)[0].astype(jnp.bfloat16)
    grad_w_fc = jnp.einsum("rd,rf->df", second_in, grad_pre, preferred_element_type=jnp.float32)
    grad_b_fc = jnp.sum(grad_pre.astype(jnp.float32), axis=0).reshape(b_fc.shape)
    grad_second_part = jnp.einsum("rf,df->rd", grad_pre, w_fc, preferred_element_type=jnp.float32)
    grad_second = lax.psum(grad_second_part, "tensor")
    grad_ln2_gain = jnp.sum(grad_second * normed_two, axis=0)
    grad_ln2_bias = jnp.sum(grad_second, axis=0)
    grad_residual = grad_float + norm_back(grad_second, normed_two, inv_two, ln2_gain)
    grad_branch = grad_residual.astype(jnp.bfloat16)
    grad_b_out = jnp.sum(grad_branch.astype(jnp.float32), axis=0)
    grad_w_out = jnp.einsum(
        "rc,rd->cd", attended, grad_branch, preferred_element_type=jnp.float32
    ).reshape(w_out.shape)
    grad_attended = (
        jnp.einsum("rd,cd->rc", grad_branch, out_matrix, preferred_element_type=jnp.float32)
        .astype(jnp.bfloat16)
        .reshape(row_count, local_heads, head_dim)
    )
    grad_query_parts = []
    grad_keys = jnp.zeros((row_count, local_heads, head_dim), jnp.float32)
    grad_values = jnp.zeros((row_count, local_heads, head_dim), jnp.float32)
    for block_index in range(block_count):
        start_row = block_index * block_rows
        end_row = start_row + block_rows
        block_queries = queries[start_row:end_row]
        scores = masked_scores(
            block_queries,
            key_rows[:end_row],
            doc_ids[start_row:end_row],
            doc_ids[:end_row],
            start_row,
            scale_factor,
        )
        attn_weights = jnp.exp(scores - log_totals[block_index])
        weights_low = attn_weights.astype(jnp.bfloat16)
        grad_rows = grad_attended[start_row:end_row]
        grad_weights = jnp.einsum(
            "qhd,khd->hqk", grad_rows, value_rows[:end_row], preferred_element_type=jnp.float32
        )
        row_delta = jnp.sum(attn_weights * grad_weights, axis=-1, keepdims=True)
        grad_scores = (attn_weights * (grad_weights - row_delta)).astype(jnp.bfloat16)
        grad_query_parts.append(
            jnp.einsum(
                "hqk,khd->qhd", grad_scores, key_rows[:end_row], preferred_element_type=jnp.float32
            )
            * scale_factor
        )
        grad_keys = grad_keys.at[:end_row].add(
            jnp.einsum(
                "hqk,qhd->khd", grad_scores, block_queries, preferred_element_type=jnp.float32
            )
            * scale_factor
        )
        grad_values = grad_values.at[:end_row].add(
            jnp.einsum("hqk,qhd->khd", weights_low, grad_rows, preferred_element_type=jnp.float32)
        )
    grad_queries = jnp.concatenate(grad_query_parts, axis=0)
    grad_mixed = jnp.stack([grad_queries, grad_keys, grad_values], axis=1).astype(jnp.bfloat16)
    grad_flat = grad_mixed.reshape(row_count, 3 * local_width)
    grad_w_qkv = jnp.einsum(
        "rd,rc->dc", first_in, grad_flat, preferred_element_type=jnp.float32
    ).reshape(w_qkv.shape)
    grad_b_qv = jnp.stack(
        [
            jnp.sum(grad_mixed[:, 0].astype(jnp.float32), axis=0),
            jnp.sum(grad_mixed[:, 2].astype(jnp.float32), axis=0),
        ],
        axis=0,
    )
    grad_first_part = jnp.einsum(
        "rc,dc->rd", grad_flat, qkv_matrix, preferred_element_type=jnp.float32
    )
    grad_first = lax.psum(grad_first_part.astype(jnp.bfloat16), "tensor").astype(jnp.float32)
    grad_ln1_gain = jnp.sum(grad_first * normed_one, axis=0)
    grad_ln1_bias = jnp.sum(grad_first, axis=0)
    grad_in = grad_residual + norm_back(grad_first, normed_one, inv_one, ln1_gain)
    shares = (
        lax.psum_scatter(grad_ln1_gain, "dp", scatter_dimension=0, tiled=True),
        lax.psum_scatter(grad_ln1_bias, "dp", scatter_dimension=0, tiled=True),
        lax.psum_scatter(grad_w_qkv, "dp", scatter_dimension=0, tiled=True),
        lax.psum_scatter(grad_b_qv, "dp", scatter_dimension=2, tiled=True),
        lax.psum_scatter(grad_w_out, "dp", scatter_dimension=2, tiled=True),
        lax.psum_scatter(grad_b_out, "dp", scatter_dimension=0, tiled=True),
        lax.psum_scatter(grad_ln2_gain, "dp", scatter_dimension=0, tiled=True),
        lax.psum_scatter(grad_ln2_bias, "dp", scatter_dimension=0, tiled=True),
        lax.psum_scatter(grad_w_fc, "dp", scatter_dimension=0, tiled=True),
        lax.psum_scatter(grad_b_fc, "dp", scatter_dimension=1, tiled=True),
        lax.psum_scatter(grad_w_proj, "dp", scatter_dimension=1, tiled=True),
        lax.psum_scatter(grad_b_proj, "dp", scatter_dimension=0, tiled=True),
    )
    return (
        block_out.astype(jnp.bfloat16),
        grad_in,
        shares[0],
        shares[1],
        shares[2],
        shares[3],
        shares[4],
        shares[5],
        shares[6],
        shares[7],
        shares[8],
        shares[9],
        shares[10],
        shares[11],
    )


def solution(mesh):
    in_specs = (
        P("dp", None),
        P("dp"),
        P(),
        P(),
        P(None, None, "tensor", None),
        P(None, "tensor", None),
        P("tensor", None, None),
        P(),
        P(),
        P(),
        P(None, "tensor"),
        P("tensor", None),
        P("tensor", None),
        P(),
        P("dp", None),
    )
    out_specs = (
        P("dp", None),
        P("dp", None),
        P("dp"),
        P("dp"),
        P("dp", None, "tensor", None),
        P(None, "tensor", "dp"),
        P("tensor", None, "dp"),
        P("dp"),
        P("dp"),
        P("dp"),
        P("dp", "tensor"),
        P("tensor", "dp"),
        P("tensor", "dp"),
        P("dp"),
    )
    return jax.shard_map(body, mesh=mesh, in_specs=in_specs, out_specs=out_specs, check_vma=False)
```

profile of v0, /device:TPU:0, one launch (start us, length us, event | category | flops | bytes accessed | tf_op | source)
XLA Modules:
  0.0 799.8 jit_solution(18134782078654954278)
XLA Ops:
  8.2 1.1 fusion.135
  9.3 2.4 convert_reduce_fusion.1
  11.7 2.9 fusion.16
  15.5 2.3 fusion.136
  18.8 1.5 fusion.139
  21.4 1.5 fusion.30
  22.9 1.5 fusion.103
  25.2 2.3 fusion.138
  27.5 1.4 fusion.5
  28.9 2.3 fusion.94
  31.2 1.0 fusion.36
  32.2 3.8 fusion.137
  36.1 1.9 fusion
  38.0 2.6 copy-done.2
  40.6 3.1 fusion.104
  43.7 3.7 convolution_bitcast_fusion
  47.9 122.0 %all-reduce.15.cloned.1.call-done = f32[2048,768]{1,0:T(8,128)} async-done(((f32[2048,768]{1,0:T(8,128)}), f32[2048,768]{1,0:T(8,128)}) %all-reduce.15.cloned.1.call-update) | async-done | bytes 6291472 | tf_op jit(solution)/shard_map/psum | solution.py:104
  170.0 4.6 fusion.132
  175.5 1.1 add_convert_fusion.1
  177.6 2.6 fusion.141
  180.7 7.7 convert_reduce_fusion.3
  188.4 1.6 copy-done.44
  190.0 4.5 fusion.142
  195.4 6.2 convolution_convert_fusion
  201.8 112.7 %all-reduce.17.cloned.1.call-done = f32[2048,768]{1,0:T(8,128)} async-done(((f32[2048,768]{1,0:T(8,128)}), f32[2048,768]{1,0:T(8,128)}) %all-reduce.17.cloned.1.call-update) | async-done | bytes 6291472 | tf_op jit(solution)/shard_map/psum | solution.py:127
  314.5 6.6 multiply_reduce_fusion.2
  321.8 5.8 convert_reduce_fusion.4
  327.7 2.1 fusion.40
  329.8 1.2 convolution_convert_fusion.1
  332.5 2.3 multiply_reduce_fusion.7
  335.0 4.2 multiply_reduce_fusion.3
  339.1 1.2 fusion.88
  341.1 5.7 multiply_reduce_fusion.1
  346.8 2.1 fusion.61
  349.1 6.4 multiply_reduce_fusion
  355.6 3.1 fusion.67
  358.7 2.9 multiply_convert_fusion.4
  362.8 3.5 multiply_convert_fusion.2
  366.3 2.1 fusion.101
  369.2 5.4 multiply_convert_fusion.1
  374.6 1.5 fusion.105
  377.1 6.3 multiply_convert_fusion
  383.4 2.0 fusion.99
  385.5 2.1 fusion.57
  387.6 1.1 fusion.102
  389.4 1.7 reshape.591
  392.2 1.4 maximum_convert_fusion
  393.6 5.5 bitcast_convert_fusion
  399.8 5.5 fusion.71
  405.3 2.8 copy.57
  408.2 6.9 fusion.143
  415.2 6.9 fusion.144
  424.1 1.4 copy.56
  425.8 29.0 %reduce-scatter.19.cloned.1.call-done = f32[96,192]{1,0:T(8,128)} async-done(((f32[768,192]{1,0:T(8,128)}), f32[96,192]{1,0:T(8,128)}) %reduce-scatter.19.cloned.1.call-update) | async-done | bytes 73744
  456.5 119.1 %all-reduce.19.cloned.1.call-done = (bf16[2048,768]{1,0:T(8,128)(2,1)}, bf16[2048,768]{1,0:T(8,128)(2,1)}) async-done(((bf16[2048,768]{1,0:T(8,128)(2,1)}, bf16[2048,768]{1,0:T(8,128)(2,1)}), (bf16[2048,768]{1,0:T(8,128)(2,1)}, bf16[2048,768]{1,0:T(8,128)(2,1)})) %all-reduce.19.cloned.1.call-update) | async-done | bytes 6291472 | tf_op jit(solution)/shard_map/psum | solution.py:117
  575.6 5.2 fusion.25
  580.9 38.1 %all-reduce.9 = (f32[768]{0:T(1024)S(1)}, f32[768]{0:T(1024)S(1)}, f32[2,3,64]{2,1,0:T(4,128)S(1)}, f32[768]{0:T(1024)S(1)}, f32[768]{0:T(1024)S(1)}, /*index=5*/f32[768]{0:T(1024)S(1)}, f32[768]{0:T(1024)S(1)}) all-reduce(f32[768]{0:T(1024)S(1)} %get-tuple-element.156, ...), channel_id=2, replica_groups=mesh['dp'=8,'tensor'=4] {'dp'}, use_global_device_ids=true, to_apply=%region_25.26.clone | all-reduce | flops 4992 | bytes 39936
  623.2 6.4 add_convert_fusion
  629.7 1.5 copy-done.12
  631.2 4.2 fusion.15
  635.4 11.5 %reduce-scatter.17.cloned.1.call-done = f32[96,576]{1,0:T(8,128)} async-done(((f32[768,576]{1,0:T(8,128)}), f32[96,576]{1,0:T(8,128)}) %reduce-scatter.17.cloned.1.call-update) | async-done | bytes 221200
  647.0 1.8 copy.58
  648.8 70.8 %reduce-scatter.13.cloned.1.call-done = f32[96,768]{1,0:T(8,128)} async-done(((f32[768,768]{1,0:T(8,128)}), f32[96,768]{1,0:T(8,128)}) %reduce-scatter.13.cloned.1.call-update) | async-done | bytes 294928 | tf_op jit(solution)/shard_map/reduce_scatter | solution.py:208
  719.6 72.9 %reduce-scatter.15.cloned.1.call-done = f32[768,96]{0,1:T(8,128)} async-done(((f32[768,768]{0,1:T(8,128)}), f32[768,96]{0,1:T(8,128)}) %reduce-scatter.15.cloned.1.call-update) | async-done | bytes 294928 | tf_op jit(solution)/shard_map/reduce_scatter | solution.py:210
  (182 shorter events, 24.0 us)
Async XLA Ops:
  7.2 173.1 %copy-start = (bf16[768,768]{1,0:T(8,128)(2,1)S(1)}, bf16[768,768]{1,0:T(8,128)(2,1)}, u32[]{:S(2)}) copy-start(bf16[768,768]{1,0:T(8,128)(2,1)} %param.47) | copy-start | bytes 3538948
  7.2 7.7 slice-start.12
  7.2 8.2 %copy-start.33 = (f32[768]{0:T(1024)S(1)}, f32[768]{0:T(1024)}, u32[]{:S(2)}) copy-start(f32[768]{0:T(1024)} %param.37) | copy-start | bytes 9220
  7.2 8.2 %copy-start.39 = (bf16[768,3,3,64]{0,3,2,1:T(8,128)(2,1)S(1)}, bf16[768,3,3,64]{0,3,2,1:T(8,128)(2,1)}, u32[]{:S(2)}) copy-start(bf16[768,3,3,64]{0,3,2,1:T(8,128)(2,1)} %param.39) | copy-start | bytes 2654212
  7.2 8.2 %copy-start.41 = (f32[768]{0:T(1024)S(1)}, f32[768]{0:T(1024)}, u32[]{:S(2)}) copy-start(f32[768]{0:T(1024)} %param.38) | copy-start | bytes 9220
  7.2 162.7 %all-reduce.15.cloned.1.call-start = ((), (), s32[]{:S(2)}) async-start(), calls=%async_computation.5 | async-start | bytes 12582912 | tf_op jit(solution)/shard_map/psum | solution.py:104
  7.3 8.2 %copy-start.7 = (bf16[2048,768]{1,0:T(8,128)(2,1)S(1)}, bf16[2048,768]{1,0:T(8,128)(2,1)}, u32[]{:S(2)}) copy-start(bf16[2048,768]{1,0:T(8,128)(2,1)} %param.35) | copy-start | bytes 9437188
  11.7 6.1 copy-start.23
  14.7 3.1 copy-start.26
  17.8 7.4 copy-start.20
  18.0 14.2 %copy-start.13 = (bf16[2048,3,64]{0,2,1:T(8,128)(2,1)}, bf16[2048,3,64]{0,2,1:T(8,128)(2,1)S(1)}, u32[]{:S(2)}) copy-start(bf16[2048,3,64]{0,2,1:T(8,128)(2,1)S(1)} %get-tuple-element.180) | copy-start | bytes 2359300
  18.8 2.6 copy-start.9
  20.3 2.6 copy-start.5
  22.9 1.5 copy-start.25
  27.5 3.7 copy-start.4
  36.1 4.5 copy-start.2
  40.6 3.1 copy-start.22
  43.7 126.2 %copy-start.37 = (f32[768]{0:T(1024)S(1)}, f32[768]{0:T(1024)}, u32[]{:S(2)}) copy-start(f32[768]{0:T(1024)} %param.42) | copy-start | bytes 9220
  47.5 267.0 %all-reduce.17.cloned.1.call-start = ((), (), s32[]{:S(2)}) async-start(), calls=%async_computation.6 | async-start | bytes 12582912 | tf_op jit(solution)/shard_map/psum | solution.py:127
  174.6 2.7 copy-start.3
  174.6 0.9 copy-start.28
  174.6 0.9 copy-start.36
  175.5 2.2 copy-start.38
  177.6 2.6 copy-start.17
  177.6 3.0 copy-start.18
  177.6 3.0 copy-start.40
  188.4 1.6 copy-start.44
  194.5 229.6 %reduce-scatter.21.cloned.1.call-start = ((), (), s32[]{:S(2)}) async-start(), calls=%async_computation.11 | async-start | bytes 73728
  201.6 253.1 %reduce-scatter.19.cloned.1.call-start = ((), (), s32[]{:S(2)}) async-start(), calls=%async_computation.10 | async-start | bytes 884736
  314.5 6.6 copy-start.11
  314.5 7.4 copy-start.19
  327.7 3.3 copy-start.6
  329.8 2.1 copy-start.10
  331.1 3.9 slice-start.6
  332.5 2.5 slice-start.7
  335.0 5.4 slice-start.3
  335.0 5.8 slice-start.4
  339.1 1.9 slice-start.5
  341.1 7.8 slice-start
  341.1 7.8 slice-start.1
  346.8 2.3 slice-start.2
  358.7 2.9 copy-start.14
  358.7 3.7 slice-start.8
  358.7 4.1 slice-start.9
  369.2 5.4 copy-start.21
  385.5 3.2 copy-start.15
  387.6 4.6 copy-start.16
  391.1 184.6 %all-reduce.19.cloned.1.call-start = ((), (), s32[]{:S(2)}) async-start(), calls=%async_computation.12 | async-start | bytes 12582912 | tf_op jit(solution)/shard_map/psum | solution.py:117
  399.1 0.7 copy-start.34
  399.1 0.7 copy-start.42
  399.1 247.9 %reduce-scatter.17.cloned.1.call-start = ((), (), s32[]{:S(2)}) async-start(), calls=%async_computation.9 | async-start | bytes 2211840
  408.1 311.4 %reduce-scatter.13.cloned.1.call-start = ((), (), s32[]{:S(2)}) async-start(), calls=%async_computation.7 | async-start | bytes 2654208 | tf_op jit(solution)/shard_map/reduce_scatter | solution.py:208
  415.1 7.0 copy-start.43
  415.2 377.4 %reduce-scatter.15.cloned.1.call-start = ((), (), s32[]{:S(2)}) async-start(), calls=%async_computation.8 | async-start | bytes 2654208 | tf_op jit(solution)/shard_map/reduce_scatter | solution.py:210
  422.1 158.7 %copy-start.29 = (f32[768]{0:T(1024)S(1)}, f32[768]{0:T(1024)}, u32[]{:S(2)}) copy-start(f32[768]{0:T(1024)} %get-tuple-element.154) | copy-start | bytes 9220
  422.1 158.7 %copy-start.30 = (f32[768]{0:T(1024)S(1)}, f32[768]{0:T(1024)}, u32[]{:S(2)}) copy-start(f32[768]{0:T(1024)} %get-tuple-element.159) | copy-start | bytes 9220
  422.1 158.7 %copy-start.31 = (f32[768]{0:T(1024)S(1)}, f32[768]{0:T(1024)}, u32[]{:S(2)}) copy-start(f32[768]{0:T(1024)} %get-tuple-element.175) | copy-start | bytes 9220
  422.1 158.7 %copy-start.32 = (f32[768]{0:T(1024)S(1)}, f32[768]{0:T(1024)}, u32[]{:S(2)}) copy-start(f32[768]{0:T(1024)} %get-tuple-element.182) | copy-start | bytes 9220
  575.6 54.0 %slice-start.10 = ((s8[6291456]{0:T(1024)(128)(4,1)}), s8[2097152]{0:T(1024)(128)(4,1)S(1)}, s32[]{:S(2)}) async-start(s8[6291456]{0:T(1024)(128)(4,1)} %bitcast.204), calls=%async_computation.23 | async-start | bytes 4194304
  623.2 6.5 slice-start.11
  623.2 6.5 copy-start.8
  623.2 8.0 %copy-start.12 = (bf16[2048,768]{1,0:T(8,128)(2,1)S(1)}, bf16[2048,768]{1,0:T(8,128)(2,1)}, u32[]{:S(2)}) copy-start(bf16[2048,768]{1,0:T(8,128)(2,1)} %get-tuple-element.172) | copy-start | bytes 9437188
  623.2 8.0 %copy-start.35 = (f32[768]{0:T(1024)S(1)}, f32[768]{0:T(1024)}, u32[]{:S(2)}) copy-start(f32[768]{0:T(1024)} %param.37) | copy-start | bytes 9220
  623.2 169.3 %copy-start.1 = (bf16[768,768]{1,0:T(8,128)(2,1)S(1)}, bf16[768,768]{1,0:T(8,128)(2,1)}, u32[]{:S(2)}) copy-start(bf16[768,768]{1,0:T(8,128)(2,1)} %param.47) | copy-start | bytes 3538948
  (2 other events, 1.4 us)
Sparse Core Ops, SparseCore 0:
  47.6 122.2 all-reduce.14
  194.7 119.7 all-reduce.16
  318.5 62.7 reduce-scatter.20
  391.2 63.4 reduce-scatter.18
  457.0 118.6 all-reduce.18
  579.0 67.9 reduce-scatter.16
  651.0 68.4 reduce-scatter.12
  723.6 68.8 reduce-scatter.14
where the time goes:
time: 809 us; the launch traced here: 800 us
  waiting for transfers between devices  538 us (67%)
  matrix products  108 us (13%)
  other arithmetic  70 us (9%)
  blocking collectives  38.1 us (5%)
  local copies, waits for them, and re-layouts  27.9 us (3%)
  between operations  16.8 us (2%)
    psum x1, waiting for transfers between devices, body(): branch = lax.psum(branch_part, 'tensor') + b_out  122 us
    psum x1, waiting for transfers between devices, body(): lax.psum(mlp_part.astype(jnp.bfloat16), 'tensor').astype(jnp.float32)  119 us
    psum x1, waiting for transfers between devices, body(): grad_second = lax.psum(grad_second_part, 'tensor')  113 us
    reduce_scatter x1, waiting for transfers between devices, body(): lax.psum_scatter(grad_w_proj, 'dp', scatter_dimension=1, tiled=True)  72.9 us
    reduce_scatter x1, waiting for transfers between devices, body(): lax.psum_scatter(grad_w_fc, 'dp', scatter_dimension=0, tiled=True)  70.8 us
    unnamed x11, waiting for transfers between devices  40.6 us
    unnamed x1, blocking collectives  38.1 us
    unnamed x132, local copies, waits for them, and re-layouts  26.4 us
  transfers between devices with their start and end apart: 8, of which 7 were waited for; matrix products, arithmetic and copies ran while one was open for 17% of the time, Pallas kernels for 0%

commit v1 on v0

--- a/solution.py
+++ b/solution.py
@@ -124,7 +124,11 @@
     grad_w_fc = jnp.einsum("rd,rf->df", second_in, grad_pre, preferred_element_type=jnp.float32)
     grad_b_fc = jnp.sum(grad_pre.astype(jnp.float32), axis=0).reshape(b_fc.shape)
     grad_second_part = jnp.einsum("rf,df->rd", grad_pre, w_fc, preferred_element_type=jnp.float32)
-    grad_second = lax.psum(grad_second_part, "tensor")
+    grad_second = grad_second_part
+    for hop in (1, 2):
+        grad_second = grad_second + lax.ppermute(
+            grad_second, "tensor", [(dev, dev ^ hop) for dev in range(4)]
+        )
     grad_ln2_gain = jnp.sum(grad_second * normed_two, axis=0)
     grad_ln2_bias = jnp.sum(grad_second, axis=0)
     grad_residual = grad_float + norm_back(grad_second, normed_two, inv_two, ln2_gain)

time: 809 us -> 837 us (1.035)
  waiting for transfers between devices: 538 us -> 565 us
    ppermute x0 -> x2, waiting for transfers between devices: none -> 140 us  [body(): lax.ppermute(grad_second, 'tensor', [(dev, dev ^ hop) for dev in range(4)])]
    psum x1 -> x0, waiting for transfers between devices: 113 us -> none  [body(): grad_second = lax.psum(grad_second_part, 'tensor')]
    unnamed x132 -> x134, local copies, waits for them, and re-layouts: 26.4 us -> 25.4 us
    unnamed x11 -> x10, waiting for transfers between devices: 40.6 us -> 40.6 us
  transfers between devices with their start and end apart: 8 -> 9, of which waited for: 7 -> 8; matrix products, arithmetic and copies ran while one was open for 17% -> 16% of each run, Pallas kernels for 0% -> 0%
where the time goes in v1:
time: 837 us; the launch traced here: 828 us
  waiting for transfers between devices  565 us (68%)
  matrix products  106 us (13%)
  other arithmetic  73.4 us (9%)
  blocking collectives  37.9 us (5%)
  local copies, waits for them, and re-layouts  26.9 us (3%)
  between operations  16.6 us (2%)
    ppermute x2, waiting for transfers between devices, body(): lax.ppermute(grad_second, 'tensor', [(dev, dev ^ hop) for dev in range(4)])  140 us
    psum x1, waiting for transfers between devices, body(): branch = lax.psum(branch_part, 'tensor') + b_out  122 us
    psum x1, waiting for transfers between devices, body(): lax.psum(mlp_part.astype(jnp.bfloat16), 'tensor').astype(jnp.float32)  119 us
    reduce_scatter x1, waiting for transfers between devices, body(): lax.psum_scatter(grad_w_proj, 'dp', scatter_dimension=1, tiled=True)  73 us
    reduce_scatter x1, waiting for transfers between devices, body(): lax.psum_scatter(grad_w_fc, 'dp', scatter_dimension=0, tiled=True)  70.5 us
    unnamed x10, waiting for transfers between devices  40.6 us
    unnamed x1, blocking collectives  37.9 us
    unnamed x134, local copies, waits for them, and re-layouts  25.4 us
  transfers between devices with their start and end apart: 9, of which 8 were waited for; matrix products, arithmetic and copies ran while one was open for 16% of the time, Pallas kernels for 0%

profile of v1, /device:TPU:0, one launch (start us, length us, event | category | flops | bytes accessed | tf_op | source)
XLA Modules:
  0.0 828.0 jit_solution(12516186542782562170)
XLA Ops:
  8.2 1.1 fusion.135
  9.3 2.4 convert_reduce_fusion.1
  11.7 2.9 fusion.16
  15.5 2.3 fusion.136
  18.8 1.4 fusion.139
  21.4 1.5 fusion.30
  22.9 1.5 fusion.103
  25.2 2.3 fusion.138
  27.5 1.4 fusion.5
  28.9 2.3 fusion.94
  32.3 3.8 fusion.137
  36.2 1.9 fusion
  38.1 2.6 copy-done.2
  40.7 3.1 fusion.104
  43.8 3.7 convolution_bitcast_fusion
  48.1 121.9 %all-reduce.14.cloned.1.call-done = f32[2048,768]{1,0:T(8,128)} async-done(((f32[2048,768]{1,0:T(8,128)}), f32[2048,768]{1,0:T(8,128)}) %all-reduce.14.cloned.1.call-update) | async-done | bytes 6291472 | tf_op jit(solution)/shard_map/psum | solution.py:104
  170.0 4.6 fusion.132
  175.6 1.1 add_convert_fusion.1
  177.7 2.7 fusion.141
  180.7 7.7 convert_reduce_fusion.3
  188.4 1.6 copy-done.43
  190.0 2.6 fusion.142
  192.8 10.1 %collective-permute-done = f32[2048,768]{1,0:T(8,128)S(1)} collective-permute-done((f32[2048,768]{1,0:T(8,128)S(1)}, f32[2048,768]{1,0:T(8,128)S(1)}, u32[]{:S(2)}, u32[]{:S(2)}) %collective-permute-start) | collective-permute-done | bytes 6291488 | tf_op jit(solution)/shard_map/ppermute | solution.py:129
  202.9 3.5 add.277
  208.0 6.3 convolution_convert_fusion
  214.4 129.9 %collective-permute-done.1 = f32[2048,768]{1,0:T(8,128)} collective-permute-done((f32[2048,768]{1,0:T(8,128)}, f32[2048,768]{1,0:T(8,128)}, u32[]{:S(2)}, u32[]{:S(2)}) %collective-permute-start.1) | collective-permute-done | bytes 6291488 | tf_op jit(solution)/shard_map/ppermute | solution.py:129
  344.3 8.7 %multiply_reduce_fusion.2 = (f32[768]{0:T(1024)}, f32[2048]{0:T(1024)S(1)}, f32[2048]{0:T(1024)S(1)}, f32[768]{0:T(1024)}, f32[2048,768]{1,0:T(8,128)S(1)}) fusion(f32[2048,768]{1,0:T(8,128)} %copy-done.3, f32[2048]{0:T(1024)S(1)} %add_rsqrt_fusion, f32[2048]{0:T(1024)S(1)} %broadcast_multiply_fusion.4, f32[768]{0:T(1024)S(1)} %copy-done.27, ...), kind=kLoop, calls=%fused_computation.51 | loop fusion | flops 15723008 | bytes 25207808 | tf_op jit(solution)/shard_map/reduce_sum | solution.py:132
  353.0 3.7 convert_reduce_fusion.4
  356.7 2.2 fusion.40
  358.9 1.2 convolution_convert_fusion.1
  361.5 2.3 multiply_reduce_fusion.7
  364.0 4.1 multiply_reduce_fusion.3
  368.1 1.2 fusion.88
  370.1 5.7 multiply_reduce_fusion.1
  375.7 2.1 fusion.61
  378.0 6.4 multiply_reduce_fusion
  384.5 3.1 fusion.67
  387.6 2.9 multiply_convert_fusion.4
  391.6 3.5 multiply_convert_fusion.2
  395.2 2.1 fusion.101
  398.0 5.4 multiply_convert_fusion.1
  403.4 1.5 fusion.105
  405.9 6.3 multiply_convert_fusion
  412.2 2.0 fusion.99
  414.3 2.1 fusion.57
  418.2 1.7 reshape.591
  420.9 1.4 maximum_convert_fusion
  422.3 5.7 bitcast_convert_fusion
  428.7 5.5 fusion.71
  434.2 2.8 copy.57
  437.1 6.9 fusion.143
  444.1 6.9 fusion.144
  453.0 1.4 copy.56
  454.7 28.9 %reduce-scatter.19.cloned.1.call-done = f32[96,192]{1,0:T(8,128)} async-done(((f32[768,192]{1,0:T(8,128)}), f32[96,192]{1,0:T(8,128)}) %reduce-scatter.19.cloned.1.call-update) | async-done | bytes 73744
  485.3 119.2 %all-reduce.16.cloned.1.call-done = (bf16[2048,768]{1,0:T(8,128)(2,1)}, bf16[2048,768]{1,0:T(8,128)(2,1)}) async-done(((bf16[2048,768]{1,0:T(8,128)(2,1)}, bf16[2048,768]{1,0:T(8,128)(2,1)}), (bf16[2048,768]{1,0:T(8,128)(2,1)}, bf16[2048,768]{1,0:T(8,128)(2,1)})) %all-reduce.16.cloned.1.call-update) | async-done | bytes 6291472 | tf_op jit(solution)/shard_map/psum | solution.py:117
  604.5 5.2 fusion.25
  609.7 37.9 %all-reduce.9 = (f32[768]{0:T(1024)S(1)}, f32[768]{0:T(1024)S(1)}, f32[2,3,64]{2,1,0:T(4,128)S(1)}, f32[768]{0:T(1024)S(1)}, f32[768]{0:T(1024)S(1)}, /*index=5*/f32[768]{0:T(1024)S(1)}, f32[768]{0:T(1024)S(1)}) all-reduce(f32[768]{0:T(1024)S(1)} %get-tuple-element.156, ...), channel_id=2, replica_groups=mesh['dp'=8,'tensor'=4] {'dp'}, use_global_device_ids=true, to_apply=%region_24.25.clone | all-reduce | flops 4992 | bytes 39936
  651.8 6.4 add_convert_fusion
  658.2 1.5 copy-done.11
  659.8 4.2 fusion.15
  664.0 11.6 %reduce-scatter.17.cloned.1.call-done = f32[96,576]{1,0:T(8,128)} async-done(((f32[768,576]{1,0:T(8,128)}), f32[96,576]{1,0:T(8,128)}) %reduce-scatter.17.cloned.1.call-update) | async-done | bytes 221200
  675.6 1.8 copy.58
  677.4 70.5 %reduce-scatter.13.cloned.1.call-done = f32[96,768]{1,0:T(8,128)} async-done(((f32[768,768]{1,0:T(8,128)}), f32[96,768]{1,0:T(8,128)}) %reduce-scatter.13.cloned.1.call-update) | async-done | bytes 294928 | tf_op jit(solution)/shard_map/reduce_scatter | solution.py:212
  747.9 73.0 %reduce-scatter.15.cloned.1.call-done = f32[768,96]{0,1:T(8,128)} async-done(((f32[768,768]{0,1:T(8,128)}), f32[768,96]{0,1:T(8,128)}) %reduce-scatter.15.cloned.1.call-update) | async-done | bytes 294928 | tf_op jit(solution)/shard_map/reduce_scatter | solution.py:214
  (187 shorter events, 25.8 us)
Async XLA Ops:
  7.2 173.2 %copy-start = (bf16[768,768]{1,0:T(8,128)(2,1)S(1)}, bf16[768,768]{1,0:T(8,128)(2,1)}, u32[]{:S(2)}) copy-start(bf16[768,768]{1,0:T(8,128)(2,1)} %param.47) | copy-start | bytes 3538948
  7.2 7.7 slice-start.14
  7.2 8.2 copy-start.32
  7.2 8.2 copy-start.38
  7.2 8.2 copy-start.40
  7.2 162.8 %all-reduce.14.cloned.1.call-start = ((), (), s32[]{:S(2)}) async-start(), calls=%async_computation.5 | async-start | bytes 12582912 | tf_op jit(solution)/shard_map/psum | solution.py:104
  7.3 8.2 copy-start.7
  11.7 6.1 copy-start.22
  14.7 3.1 copy-start.25
  17.8 7.4 copy-start.19
  18.0 14.3 %copy-start.12 = (bf16[2048,3,64]{0,2,1:T(8,128)(2,1)}, bf16[2048,3,64]{0,2,1:T(8,128)(2,1)S(1)}, u32[]{:S(2)}) copy-start(bf16[2048,3,64]{0,2,1:T(8,128)(2,1)S(1)} %get-tuple-element.181) | copy-start | bytes 2359300
  18.8 2.6 copy-start.9
  20.3 2.6 copy-start.5
  22.9 1.5 copy-start.24
  27.5 3.7 copy-start.4
  36.1 4.5 copy-start.2
  40.7 3.1 copy-start.21
  43.8 126.2 %copy-start.36 = (f32[768]{0:T(1024)S(1)}, f32[768]{0:T(1024)}, u32[]{:S(2)}) copy-start(f32[768]{0:T(1024)} %param.42) | copy-start | bytes 9220
  47.5 405.5 %reduce-scatter.21.cloned.1.call-start = ((), (), s32[]{:S(2)}) async-start(), calls=%async_computation.10 | async-start | bytes 73728
  174.6 2.7 copy-start.3
  174.6 0.9 copy-start.27
  174.6 0.9 copy-start.35
  175.5 2.2 copy-start.37
  177.7 2.7 copy-start.16
  177.7 3.0 copy-start.17
  177.7 3.0 copy-start.39
  188.4 1.6 copy-start.43
  192.7 10.2 %collective-permute-start = (f32[2048,768]{1,0:T(8,128)S(1)}, f32[2048,768]{1,0:T(8,128)S(1)}, u32[]{:S(2)}, u32[]{:S(2)}) collective-permute-start(f32[2048,768]{1,0:T(8,128)S(1)} %fusion.142), channel_id=1, source_target_pairs={{0,1},{1,0},{2,3},{3,2},{4,5},{5,4},{6,7},{7,6},{8,9},{9,8},{10,11... | collective-permute-start | bytes 18874376 | tf_op jit(solution)/shard_map/ppermute | solution.py:129
  206.4 137.9 %collective-permute-start.1 = (f32[2048,768]{1,0:T(8,128)}, f32[2048,768]{1,0:T(8,128)}, u32[]{:S(2)}, u32[]{:S(2)}) collective-permute-start(f32[2048,768]{1,0:T(8,128)} %add.277), channel_id=1, source_target_pairs={{0,2},{1,3},{2,0},{3,1},{4,6},{5,7},{6,4},{7,5},{8,10},{9,11},{10,... | collective-permute-start | bytes 18874376 | tf_op jit(solution)/shard_map/ppermute | solution.py:129
  207.8 275.8 %reduce-scatter.19.cloned.1.call-start = ((), (), s32[]{:S(2)}) async-start(), calls=%async_computation.9 | async-start | bytes 884736
  208.0 145.0 %slice-start.3 = ((s8[6291456]{0:T(1024)(128)(4,1)}), s8[4194304]{0:T(1024)(128)(4,1)S(1)}, s32[]{:S(2)}) async-start(s8[6291456]{0:T(1024)(128)(4,1)} %bitcast.198), calls=%async_computation.15 | async-start | bytes 8388608
  214.4 138.6 %slice-start.4 = ((s8[6291456]{0:T(1024)(128)(4,1)}), s8[2097152]{0:T(1024)(128)(4,1)S(1)}, s32[]{:S(2)}) async-start(s8[6291456]{0:T(1024)(128)(4,1)} %bitcast.198), calls=%async_computation.16 | async-start | bytes 4194304
  214.4 138.6 %copy-start.18 = (bf16[2048,768]{1,0:T(8,128)(2,1)S(1)}, bf16[2048,768]{1,0:T(8,128)(2,1)}, u32[]{:S(2)}) copy-start(bf16[2048,768]{1,0:T(8,128)(2,1)} %param.49) | copy-start | bytes 9437188
  356.7 3.4 copy-start.6
  358.9 2.0 copy-start.10
  360.1 3.8 slice-start.8
  361.5 2.5 slice-start.9
  364.0 5.4 slice-start.5
  364.0 5.7 slice-start.6
  368.1 1.9 slice-start.7
  370.1 7.8 slice-start
  370.1 7.8 slice-start.1
  375.7 2.3 slice-start.2
  387.6 2.9 copy-start.13
  387.6 3.7 slice-start.10
  387.6 4.0 slice-start.11
  398.0 5.4 copy-start.20
  414.3 3.2 copy-start.14
  416.4 4.6 copy-start.15
  419.9 184.6 %all-reduce.16.cloned.1.call-start = ((), (), s32[]{:S(2)}) async-start(), calls=%async_computation.11 | async-start | bytes 12582912 | tf_op jit(solution)/shard_map/psum | solution.py:117
  428.0 247.5 %reduce-scatter.17.cloned.1.call-start = ((), (), s32[]{:S(2)}) async-start(), calls=%async_computation.8 | async-start | bytes 2211840
  437.1 310.9 %reduce-scatter.13.cloned.1.call-start = ((), (), s32[]{:S(2)}) async-start(), calls=%async_computation.6 | async-start | bytes 2654208 | tf_op jit(solution)/shard_map/reduce_scatter | solution.py:212
  444.0 7.0 copy-start.42
  444.1 376.9 %reduce-scatter.15.cloned.1.call-start = ((), (), s32[]{:S(2)}) async-start(), calls=%async_computation.7 | async-start | bytes 2654208 | tf_op jit(solution)/shard_map/reduce_scatter | solution.py:214
  451.0 158.6 %copy-start.28 = (f32[768]{0:T(1024)S(1)}, f32[768]{0:T(1024)}, u32[]{:S(2)}) copy-start(f32[768]{0:T(1024)} %get-tuple-element.154) | copy-start | bytes 9220
  451.1 158.6 %copy-start.29 = (f32[768]{0:T(1024)S(1)}, f32[768]{0:T(1024)}, u32[]{:S(2)}) copy-start(f32[768]{0:T(1024)} %get-tuple-element.159) | copy-start | bytes 9220
  451.1 158.6 %copy-start.30 = (f32[768]{0:T(1024)S(1)}, f32[768]{0:T(1024)}, u32[]{:S(2)}) copy-start(f32[768]{0:T(1024)} %get-tuple-element.175) | copy-start | bytes 9220
  451.1 158.6 %copy-start.31 = (f32[768]{0:T(1024)S(1)}, f32[768]{0:T(1024)}, u32[]{:S(2)}) copy-start(f32[768]{0:T(1024)} %get-tuple-element.183) | copy-start | bytes 9220
  604.5 53.7 %slice-start.12 = ((s8[6291456]{0:T(1024)(128)(4,1)}), s8[2097152]{0:T(1024)(128)(4,1)S(1)}, s32[]{:S(2)}) async-start(s8[6291456]{0:T(1024)(128)(4,1)} %bitcast.206), calls=%async_computation.24 | async-start | bytes 4194304
  651.7 6.5 slice-start.13
  651.7 6.5 copy-start.8
  651.7 8.0 copy-start.11
  651.8 8.0 copy-start.34
  651.8 169.2 %copy-start.1 = (bf16[768,768]{1,0:T(8,128)(2,1)S(1)}, bf16[768,768]{1,0:T(8,128)(2,1)}, u32[]{:S(2)}) copy-start(bf16[768,768]{1,0:T(8,128)(2,1)} %param.47) | copy-start | bytes 3538948
  (4 other events, 2.9 us)
Sparse Core Ops, SparseCore 0:
  47.7 122.2 all-reduce.13
  207.9 63.3 reduce-scatter.20
  420.0 63.5 reduce-scatter.18
  485.8 118.6 all-reduce.15
  607.8 67.7 reduce-scatter.16
  679.5 68.3 reduce-scatter.12
  752.0 68.9 reduce-scatter.14
